TPU v7x, 32 devices: a whole 2x2x4 slice. The times are simulated.
32 devices in a mesh: groups: 1, samp: 4 (over x, core), var: 8 (over z, y).
Axes of the slice: x: 2, y: 2, z: 4, core: 2. Of those that a mesh axis runs over, the one named last changes fastest.
Arguments:
- expression: bfloat16 [4096, 5120], P(('groups', 'samp'), 'var'), may hold values from -6 to 6
- genotypes: bfloat16 [4096, 1536], P(('groups', 'samp'), 'var'), may hold values from 0 to 2
- covariates: bfloat16 [4096, 64], P(('groups', 'samp')), may hold values from -6 to 6
- distance_bins: int32 [24, 5120], P('groups', ('var', 'samp')), may hold values from 0 to 15
- gene_folds: int32 [5120], P(('groups', 'var', 'samp')), may hold values from 0 to 4
- fold_weights: float32 [5, 16], replicated, may hold values from 0.25 to 4
Outputs:
- weighted_stats: float32 [5120, 1536], P(('groups', 'var', 'samp'))
Inputs may be any that keep to these rules, and one draw needn't show every extreme that they name: `distance_bins`: bins index rows of fold_weights' second dimension. `gene_folds`: folds index rows of fold_weights.
All inputs are finite; a program needn't handle non-finite values.
Results may differ from a plain program's by a relative error of at most 0.0047.
Values may be sent and summed in bfloat16 or wider, within the bound.
A program may use at most 64 MiB of HBM per device.

v0:
```python
import jax
import jax.numpy as jnp
from jax import lax
from jax.sharding import PartitionSpec as P

COVS = 64
VARS = 1536
VTILE = 64
NBINS = 16
FOLDS = 5
VTILES = 24


def solve_fit(data, design, factor, cross):
    beta = jax.scipy.linalg.cho_solve((factor, True), cross)
    fitted = jnp.dot(design.astype(jnp.float32), beta, precision=lax.Precision.HIGHEST)
    return (beta, data.astype(jnp.float32) - fitted)


def shards(expression, genotypes, covariates, distance_bins, gene_folds, fold_weights):
    sample_rows = expression.shape[0]
    samples = sample_rows * lax.axis_size("samp")
    design = jnp.concatenate([jnp.ones((sample_rows, 1), jnp.bfloat16), covariates], axis=1)
    source = lax.all_gather(genotypes, "var", axis=1, tiled=True)
    gram = jnp.dot(design.T, design, preferred_element_type=jnp.float32)
    expr_cross = jnp.dot(design.T, expression, preferred_element_type=jnp.float32)
    geno_cross = jnp.dot(design.T, source, preferred_element_type=jnp.float32)
    partial_sums = (gram, expr_cross, geno_cross)
    summed = lax.psum((partial_sums[0], partial_sums[1], partial_sums[2]), "samp")
    gram, expr_cross, geno_cross = (summed[0], summed[1], summed[2])
    factor = jnp.linalg.cholesky(gram)
    expr_beta, expr_resid = solve_fit(expression, design, factor, expr_cross)
    geno_beta, geno_resid = solve_fit(source, design, factor, geno_cross)
    expr_norm, geno_norm = lax.psum(
        (jnp.sum(expr_resid * expr_resid, axis=0), jnp.sum(geno_resid * geno_resid, axis=0)), "samp"
    )
    expr_unit = (expr_resid * lax.rsqrt(expr_norm + 1e-06)).astype(jnp.bfloat16)
    geno_unit = (geno_resid * lax.rsqrt(geno_norm + 1e-06)).astype(jnp.bfloat16)
    terms = lax.dot_general(
        expr_unit, geno_unit, (((0,), (0,)), ((), ())), preferred_element_type=jnp.float32
    )
    corr = lax.psum_scatter(terms, "samp", scatter_dimension=0, tiled=True)
    local_genes = corr.shape[0]
    fold_onehot = (gene_folds[:, None] == jnp.arange(FOLDS)[None, :]).astype(jnp.float32)
    row_weights = jnp.dot(fold_onehot, fold_weights, precision=lax.Precision.HIGHEST)
    bin_match = distance_bins.T[:, :, None] == jnp.arange(NBINS)[None, None, :]
    tile_weight = jnp.sum(jnp.where(bin_match, row_weights[:, None, :], 0.0), axis=2)
    dof = jnp.float32(samples - COVS - 2)
    stats = dof * corr * corr
    weighted = stats.reshape(local_genes, VTILES, VTILE) * tile_weight[:, :, None]
    return weighted.reshape(local_genes, VARS)


def solution(mesh):
    return jax.shard_map(
        shards,
        mesh=mesh,
        in_specs=(
            P(("groups", "samp"), "var"),
            P(("groups", "samp"), "var"),
            P(("groups", "samp"), None),
            P("groups", ("var", "samp")),
            P(("groups", "var", "samp")),
            P(),
        ),
        out_specs=P(("groups", "var", "samp"), None),
        check_vma=False,
    )
```

profile of v0, /device:TPU:0, one launch (start us, length us, event | category | flops | bytes accessed | tf_op | source)
XLA Modules:
  0.0 191.9 jit_solution(71797673533566679)
XLA Ops:
  6.5 0.7 all-gather.2.cloned.1.call-update
  7.3 1.2 fusion.11
  8.5 13.2 %psum.35 = f32[65,65]{0,1:T(8,128)S(1)} all-reduce(f32[65,65]{0,1:T(8,128)S(1)} %fusion.11), channel_id=1, replica_groups=mesh['groups'=1,'samp'=4,'var'=8] {'samp'}, use_global_device_ids=true, to_apply=%region_0.0 | all-reduce | flops 4225 | bytes 33800 | tf_op jit(solution)/shard_map/psum | solution.py:29
  21.8 5.9 %cholesky.16 = f32[65,65]{1,0:T(8,128)S(1)} custom-call(f32[65,65]{1,0:T(8,128)S(1)} %fusion.24), custom_call_target="Cholesky" | custom-call | tf_op jit(solution)/shard_map/jit(cholesky)/cholesky | solution.py:31
  27.8 2.4 %fusion.9 = f32[65,640]{1,0:T(8,128)} fusion(bf16[1024,640]{1,0:T(8,128)(2,1)} %param.6, bf16[1024,64]{0,1:T(8,128)(2,1)} %param.8), kind=kOutput, calls=%fused_computation.18 | convolution fusion | flops 85196800 | bytes 1608192 | tf_op jit(solution)/shard_map/dot_general | solution.py:26
  30.2 42.2 %all-gather.2.cloned.1.call-done = bf16[1024,1536]{0,1:T(8,128)(2,1)} async-done(((bf16[1024,192]{0,1:T(8,128)(2,1)}), bf16[1024,1536]{0,1:T(8,128)(2,1)}) %all-gather.2.cloned.1.call-update) | async-done | bytes 3145744 | tf_op jit(solution)/shard_map/all_gather | solution.py:24
  72.4 4.0 %fusion.5 = f32[65,1536]{1,0:T(8,128)} fusion(bf16[1024,1536]{0,1:T(8,128)(2,1)} %all-gather.2.cloned.1.call-done, bf16[1024,64]{0,1:T(8,128)(2,1)} %param.8), kind=kOutput, calls=%fused_computation.14 | convolution fusion | flops 204472320 | bytes 3676160 | tf_op jit(solution)/shard_map/dot_general | solution.py:27
  76.4 0.7 compare_reduce_fusion
  77.1 0.6 fusion.15
  77.7 5.0 %custom-call.16 = f32[1,65,65]{1,2,0:T(8,128)S(1)} custom-call(f32[1,65,65]{2,1,0:T(8,128)S(1)} %fusion.15), custom_call_target="InvertDiagBlocksLowerTriangular" | custom-call | tf_op jit(solution)/shard_map/jit(_cho_solve)/triangular_solve | solution.py:15
  82.7 3.0 %copy.24 = bf16[1024,1536]{1,0:T(8,128)(2,1)} copy(bf16[1024,1536]{0,1:T(8,128)(2,1)S(1)} %copy-done.1) | data formatting | bytes 6291456 | tf_op jit(solution)/shard_map/all_gather | solution.py:24
  85.7 23.3 %all-reduce.5.cloned.1.call-done = (f32[65,1536]{1,0:T(8,128)}, f32[65,640]{1,0:T(8,128)}) async-done(((f32[65,1536]{1,0:T(8,128)}, f32[65,640]{1,0:T(8,128)}), (f32[65,1536]{1,0:T(8,128)}, f32[65,640]{1,0:T(8,128)})) %all-reduce.5.cloned.1.call-update) | async-done | bytes 565776 | tf_op jit(solution)/shard_map/psum | solution.py:29
  108.9 1.6 fusion.18
  110.5 0.5 fusion.16
  111.1 1.4 fusion.22
  112.9 3.0 %multiply_reduce_fusion.1 = (f32[640]{0:T(1024)S(1)}, f32[1024,640]{1,0:T(8,128)}) fusion(bf16[1024,640]{1,0:T(8,128)(2,1)S(1)} %copy-done.3, f32[65,640]{1,0:T(8,128)S(1)} %fusion.20, bf16[1024,64]{0,1:T(8,128)(2,1)S(1)} %copy-done.4), kind=kOutput, calls=%fused_computation.6 | convolution fusion | flops 513801600 | bytes 4232192 | tf_op jit(solution)/shard_map/dot_general | solution.py:16
  115.8 5.1 %multiply_reduce_fusion = (f32[1536]{0:T(1024)S(1)}, f32[1024,1536]{1,0:T(8,128)}) fusion(f32[65,1536]{1,0:T(8,128)S(1)} %fusion.16, bf16[1024,64]{0,1:T(8,128)(2,1)S(1)} %copy-done.4, bf16[1024,1536]{1,0:T(8,128)(2,1)S(1)} %copy-done.2), kind=kOutput, calls=%fused_computation.1 | convolution fusion | flops 1233123840 | bytes 9973760 | tf_op jit(solution)/shard_map/dot_general | solution.py:16
  120.9 10.3 %all-reduce.1 = (f32[1536]{0:T(1024)S(1)}, f32[640]{0:T(1024)S(1)}) all-reduce(f32[1536]{0:T(1024)S(1)} %get-tuple-element.9, f32[640]{0:T(1024)S(1)} %get-tuple-element.11), channel_id=1, replica_groups=mesh['groups'=1,'samp'=4,'var'=8] {'samp'}, use_global_device_ids=true, to_apply=%region_8.9 | all-reduce | flops 2176 | bytes 17408 | tf_op jit(solution)/shard_map/psum | solution.py:34
  131.2 7.9 %fusion = f32[640,1536]{1,0:T(8,128)} fusion(f32[1024,1536]{1,0:T(8,128)} %get-tuple-element.10, f32[1536]{0:T(1024)S(1)} %add_rsqrt_fusion, f32[1024,640]{1,0:T(8,128)} %get-tuple-element.12, bf16[1024,640]{1,0:T(8,128)(2,1)S(1)} %copy-done.3, f32[640]{0:T(1024)S(1)} %add_rsqrt_fusion.1), kind=kOutput, calls=%fused_computation.3 | convolution fusion | flops 2019033088 | bytes 14164480 | tf_op jit(solution)/shard_map/dot_general | solution.py:39
  139.1 0.6 copy-done.6
  140.2 0.6 mul.51
  140.8 0.5 mul.52
  141.3 41.7 %reduce-scatter.2.cloned.1.call-done = f32[160,1536]{1,0:T(8,128)} async-done(((f32[640,1536]{1,0:T(8,128)}), f32[160,1536]{1,0:T(8,128)}) %reduce-scatter.2.cloned.1.call-update) | async-done | bytes 983056 | tf_op jit(solution)/shard_map/reduce_scatter | solution.py:42
  183.0 2.3 %fusion.3 = f32[160,1536]{1,0:T(8,128)} fusion(f32[160,1536]{1,0:T(8,128)S(1)} %mul.52, f32[160,1536]{1,0:T(8,128)} %reduce-scatter.2.cloned.1.call-done), kind=kLoop, calls=%fused_computation.10 | loop fusion | flops 737280 | bytes 2949120 | tf_op jit(solution)/shard_map/mul | solution.py:50
  (27 shorter events, 1.1 us)
Async XLA Ops:
  6.5 132.6 %copy-start = (f32[5,16]{1,0:T(8,128)S(1)}, f32[5,16]{1,0:T(8,128)}, u32[]{:S(2)}) copy-start(f32[5,16]{1,0:T(8,128)} %param.11) | copy-start | bytes 964
  6.5 65.8 %all-gather.2.cloned.1.call-start = ((), (), s32[]{:S(2)}) async-start(), calls=%async_computation.1 | async-start | bytes 3538944 | tf_op jit(solution)/shard_map/all_gather | solution.py:24
  7.3 101.7 %all-reduce.5.cloned.1.call-start = ((), (), s32[]{:S(2)}) async-start(), calls=%async_computation.3 | async-start | bytes 1253376 | tf_op jit(solution)/shard_map/psum | solution.py:29
  72.4 10.3 %copy-start.1 = (bf16[1024,1536]{0,1:T(8,128)(2,1)S(1)}, bf16[1024,1536]{0,1:T(8,128)(2,1)}, u32[]{:S(2)}) copy-start(bf16[1024,1536]{0,1:T(8,128)(2,1)} %all-gather.2.cloned.1.call-done) | copy-start | bytes 9437188
  76.3 106.7 %reduce-scatter.2.cloned.1.call-start = ((), (), s32[]{:S(2)}) async-start(), calls=%async_computation.2 | async-start | bytes 4915200 | tf_op jit(solution)/shard_map/reduce_scatter | solution.py:42
  85.7 27.2 %copy-start.3 = (bf16[1024,640]{1,0:T(8,128)(2,1)S(1)}, bf16[1024,640]{1,0:T(8,128)(2,1)}, u32[]{:S(2)}) copy-start(bf16[1024,640]{1,0:T(8,128)(2,1)} %param.6) | copy-start | bytes 3932164
  85.7 27.2 %copy-start.4 = (bf16[1024,64]{0,1:T(8,128)(2,1)S(1)}, bf16[1024,64]{0,1:T(8,128)(2,1)}, u32[]{:S(2)}) copy-start(bf16[1024,64]{0,1:T(8,128)(2,1)} %param.8) | copy-start | bytes 393220
  111.0 4.8 %copy-start.2 = (bf16[1024,1536]{1,0:T(8,128)(2,1)S(1)}, bf16[1024,1536]{1,0:T(8,128)(2,1)}, u32[]{:S(2)}) copy-start(bf16[1024,1536]{1,0:T(8,128)(2,1)} %copy.24) | copy-start | bytes 9437188
  139.1 0.7 copy-start.6
  139.1 0.9 copy-start.5
Sparse Core Ops, SparseCore 0:
  9.5 62.8 all-gather.1
  76.5 32.4 all-reduce.4
  139.2 43.7 reduce-scatter.1
where the time goes:
time: 192 us
  waiting for transfers between devices  108 us (56%)
  matrix products  27.5 us (14%)
  blocking collectives  23.5 us (12%)
  other arithmetic  14.7 us (8%)
  between operations  13.2 us (7%)
  local copies, waits for them, and re-layouts  4.89 us (3%)
    all_gather x1, waiting for transfers between devices, shards(): source = lax.all_gather(genotypes, 'var', axis=1, tiled=True)  42.2 us
    reduce_scatter x1, waiting for transfers between devices, shards(): corr = lax.psum_scatter(terms, 'samp', scatter_dimension=0, tiled=True)  41.7 us
    psum x1, waiting for transfers between devices, shards(): lax.psum((partial_sums[0], partial_sums[1], partial_sums[2]), 'samp')  23.3 us
    psum x1, blocking collectives, shards(): lax.psum((partial_sums[0], partial_sums[1], partial_sums[2]), 'samp')  13.2 us
    psum x1, blocking collectives, shards(): lax.psum((jnp.sum(expr_resid * expr_resid, axis=0), jnp.sum(geno_resid *...  10.3 us
    dot_general x2, matrix products, solve_fit(): jnp.dot(design.astype(jnp.float32), beta, precision=lax.Precision.HIGHEST)  8.05 us
    dot_general x1, matrix products, shards(): lax.dot_general(expr_unit, geno_unit, (((0,), (0,)), ((), ())), preferred...  7.86 us
    another operation x3, other arithmetic, shards(): factor = jnp.linalg.cholesky(gram)  6.64 us
  transfers between devices with their start and end apart: 3, of which 3 were waited for; matrix products, arithmetic and copies ran while one was open for 11% of the time, Pallas kernels for 0%

commit v1 on v0

--- a/solution.py
+++ b/solution.py
@@ -21,7 +21,12 @@
     sample_rows = expression.shape[0]
     samples = sample_rows * lax.axis_size("samp")
     design = jnp.concatenate([jnp.ones((sample_rows, 1), jnp.bfloat16), covariates], axis=1)
-    source = lax.all_gather(genotypes, "var", axis=1, tiled=True)
+    ring = [genotypes]
+    for hop in range(7):
+        ring.append(lax.ppermute(ring[-1], "var", [(dev, (dev + 1) % 8) for dev in range(8)]))
+    source = jnp.roll(
+        jnp.concatenate(ring[::-1], axis=1), (lax.axis_index("var") + 1) * ring[0].shape[1], axis=1
+    )
     gram = jnp.dot(design.T, design, preferred_element_type=jnp.float32)
     expr_cross = jnp.dot(design.T, expression, preferred_element_type=jnp.float32)
     geno_cross = jnp.dot(design.T, source, preferred_element_type=jnp.float32)

time: 192 us -> 245 us (1.28)
  waiting for transfers between devices: 108 us -> 148 us
  local copies, waits for them, and re-layouts: 4.89 us -> 13.7 us
  starting transfers between devices: 0.08 us -> 3.11 us
    ppermute x0 -> x7, waiting for transfers between devices: none -> 81.1 us  [shards(): lax.ppermute(ring[-1], 'var', [(dev, (dev + 1) % 8) for dev in range(8)])]
    all_gather x1 -> x0, waiting for transfers between devices: 42.2 us -> none  [shards(): source = lax.all_gather(genotypes, 'var', axis=1, tiled=True)]
    concatenate x0 -> x1, local copies, waits for them, and re-layouts: none -> 10.6 us  [shards(): jnp.roll(jnp.concatenate(ring[::-1], axis=1), (lax.axis_index('var') + 1)...]
    ppermute x0 -> x7, starting transfers between devices: none -> 3.06 us  [shards(): lax.ppermute(ring[-1], 'var', [(dev, (dev + 1) % 8) for dev in range(8)])]
    all_gather x1 -> x0, local copies, waits for them, and re-layouts: 2.97 us -> none  [shards(): source = lax.all_gather(genotypes, 'var', axis=1, tiled=True)]
  transfers between devices with their start and end apart: 3 -> 9, of which waited for: 3 -> 9; matrix products, arithmetic and copies ran while one was open for 11% -> 7% of each run, Pallas kernels for 0% -> 0%
where the time goes in v1:
time: 245 us; the launch traced here: 243 us
  waiting for transfers between devices  148 us (60%)
  matrix products  29.5 us (12%)
  blocking collectives  21.2 us (9%)
  other arithmetic  14.9 us (6%)
  local copies, waits for them, and re-layouts  13.7 us (6%)
  between operations  13.6 us (6%)
  starting transfers between devices  3.11 us (1%)
    ppermute x7, waiting for transfers between devices, shards(): lax.ppermute(ring[-1], 'var', [(dev, (dev + 1) % 8) for dev in range(8)])  81.1 us
    reduce_scatter x1, waiting for transfers between devices, shards(): corr = lax.psum_scatter(terms, 'samp', scatter_dimension=0, tiled=True)  41.2 us
    psum x1, waiting for transfers between devices, shards(): lax.psum((partial_sums[0], partial_sums[1], partial_sums[2]), 'samp')  25.2 us
    psum x1, blocking collectives, shards(): lax.psum((partial_sums[0], partial_sums[1], partial_sums[2]), 'samp')  10.9 us
    concatenate x1, local copies, waits for them, and re-layouts, shards(): jnp.roll(jnp.concatenate(ring[::-1], axis=1), (lax.axis_index('var') + 1)...  10.6 us
    psum x1, blocking collectives, shards(): lax.psum((jnp.sum(expr_resid * expr_resid, axis=0), jnp.sum(geno_resid *...  10.3 us
    dot_general x2, matrix products, solve_fit(): jnp.dot(design.astype(jnp.float32), beta, precision=lax.Precision.HIGHEST)  10.1 us
    dot_general x1, matrix products, shards(): lax.dot_general(expr_unit, geno_unit, (((0,), (0,)), ((), ())), preferred...  8.92 us
  transfers between devices with their start and end apart: 9, of which 9 were waited for; matrix products, arithmetic and copies ran while one was open for 7% of the time, Pallas kernels for 0%

profile of v1, /device:TPU:0, one launch (start us, length us, event | category | flops | bytes accessed | tf_op | source)
XLA Modules:
  0.0 243.4 jit_solution(11741288086791719827)
XLA Ops:
  6.5 1.2 copy.23
  7.8 3.0 %collective-permute-start = (bf16[1024,192]{1,0:T(8,128)(2,1)S(1)}, bf16[1024,192]{1,0:T(8,128)(2,1)S(1)}, u32[]{:S(2)}, u32[]{:S(2)}) collective-permute-start(bf16[1024,192]{1,0:T(8,128)(2,1)S(1)} %copy.23), channel_id=1, source_target_pairs={{0,1},{1,2},{2,3},{3,4},{4,5},{5,6},{6,7},{7,0},{8,9},{9,10},{10,1... | collective-permute-start | bytes 1179656 | tf_op jit(solution)/shard_map/ppermute | solution.py:26
  10.8 15.0 %collective-permute-done = bf16[1024,192]{1,0:T(8,128)(2,1)S(1)} collective-permute-done((bf16[1024,192]{1,0:T(8,128)(2,1)S(1)}, bf16[1024,192]{1,0:T(8,128)(2,1)S(1)}, u32[]{:S(2)}, u32[]{:S(2)}) %collective-permute-start) | collective-permute-done | bytes 393248 | tf_op jit(solution)/shard_map/ppermute | solution.py:26
  25.8 15.8 %collective-permute-done.1 = bf16[1024,192]{1,0:T(8,128)(2,1)S(1)} collective-permute-done((bf16[1024,192]{1,0:T(8,128)(2,1)S(1)}, bf16[1024,192]{1,0:T(8,128)(2,1)S(1)}, u32[]{:S(2)}, u32[]{:S(2)}) %collective-permute-start.1) | collective-permute-done | bytes 393248 | tf_op jit(solution)/shard_map/ppermute | solution.py:26
  41.6 14.9 %collective-permute-done.2 = bf16[1024,192]{1,0:T(8,128)(2,1)S(1)} collective-permute-done((bf16[1024,192]{1,0:T(8,128)(2,1)S(1)}, bf16[1024,192]{1,0:T(8,128)(2,1)S(1)}, u32[]{:S(2)}, u32[]{:S(2)}) %collective-permute-start.2) | collective-permute-done | bytes 393248 | tf_op jit(solution)/shard_map/ppermute | solution.py:26
  56.5 14.1 %collective-permute-done.3 = bf16[1024,192]{1,0:T(8,128)(2,1)S(1)} collective-permute-done((bf16[1024,192]{1,0:T(8,128)(2,1)S(1)}, bf16[1024,192]{1,0:T(8,128)(2,1)S(1)}, u32[]{:S(2)}, u32[]{:S(2)}) %collective-permute-start.3) | collective-permute-done | bytes 393248 | tf_op jit(solution)/shard_map/ppermute | solution.py:26
  70.6 13.2 %collective-permute-done.4 = bf16[1024,192]{1,0:T(8,128)(2,1)S(1)} collective-permute-done((bf16[1024,192]{1,0:T(8,128)(2,1)S(1)}, bf16[1024,192]{1,0:T(8,128)(2,1)S(1)}, u32[]{:S(2)}, u32[]{:S(2)}) %collective-permute-start.4) | collective-permute-done | bytes 393248 | tf_op jit(solution)/shard_map/ppermute | solution.py:26
  83.8 1.2 fusion.14
  85.0 10.9 %psum.35 = f32[65,65]{0,1:T(8,128)S(1)} all-reduce(f32[65,65]{0,1:T(8,128)S(1)} %fusion.14), channel_id=1, replica_groups=mesh['groups'=1,'samp'=4,'var'=8] {'samp'}, use_global_device_ids=true, to_apply=%region_0.1 | all-reduce | flops 4225 | bytes 33800 | tf_op jit(solution)/shard_map/psum | solution.py:34
  96.3 5.9 %cholesky.16 = f32[65,65]{1,0:T(8,128)S(1)} custom-call(f32[65,65]{1,0:T(8,128)S(1)} %fusion.27), custom_call_target="Cholesky" | custom-call | tf_op jit(solution)/shard_map/jit(cholesky)/cholesky | solution.py:36
  102.3 2.4 fusion.12
  104.7 7.9 %collective-permute-done.6 = bf16[1024,192]{1,0:T(8,128)(2,1)} collective-permute-done((bf16[1024,192]{1,0:T(8,128)(2,1)}, bf16[1024,192]{1,0:T(8,128)(2,1)}, u32[]{:S(2)}, u32[]{:S(2)}) %collective-permute-start.6) | collective-permute-done | bytes 393248 | tf_op jit(solution)/shard_map/ppermute | solution.py:26
  112.5 10.6 %concatenate.10 = bf16[1024,3072]{1,0:T(8,128)(2,1)} concatenate(bf16[1024,192]{1,0:T(8,128)(2,1)} %collective-permute-done.6, bf16[1024,192]{1,0:T(8,128)(2,1)} %collective-permute-done.5, bf16[1024,192]{1,0:T(8,128)(2,1)S(1)} %collective-permute-done.4, bf16[1024,192]{1,0:T(8,128)(2,1)S(1)} %collective-permute-done.3, bf16[1024,192]{1,0:T(8,128)(2,1)S(1)} %collective-permute-done.2, ...), dimensions={1} | concatenate | bytes 12582912 | tf_op jit(solution)/shard_map/jit(_roll_dynamic)/concatenate | solution.py:27
  123.1 3.9 %fusion.3 = f32[65,1536]{1,0:T(8,128)} fusion(bf16[1024,3072]{1,0:T(8,128)(2,1)} %concatenate.10, s32[]{:T(128)S(6)} %select_n.23, bf16[1024,64]{0,1:T(8,128)(2,1)S(1)} %copy-done.2), kind=kOutput, calls=%fused_computation.9 | convolution fusion | flops 204472320 | bytes 3676164 | tf_op jit(solution)/shard_map/dot_general | solution.py:32
  127.1 0.7 compare_reduce_fusion
  128.5 5.0 %custom-call.16 = f32[1,65,65]{1,2,0:T(8,128)S(1)} custom-call(f32[1,65,65]{2,1,0:T(8,128)S(1)} %fusion.18), custom_call_target="InvertDiagBlocksLowerTriangular" | custom-call | tf_op jit(solution)/shard_map/jit(_cho_solve)/triangular_solve | solution.py:15
  133.5 25.2 %all-reduce.5.cloned.1.call-done = (f32[65,1536]{1,0:T(8,128)}, f32[65,640]{1,0:T(8,128)}) async-done(((f32[65,1536]{1,0:T(8,128)}, f32[65,640]{1,0:T(8,128)}), (f32[65,1536]{1,0:T(8,128)}, f32[65,640]{1,0:T(8,128)})) %all-reduce.5.cloned.1.call-update) | async-done | bytes 565776 | tf_op jit(solution)/shard_map/psum | solution.py:34
  158.6 1.6 fusion.21
  160.8 7.1 %multiply_reduce_fusion = (f32[1536]{0:T(1024)S(1)}, f32[1024,1536]{1,0:T(8,128)}) fusion(bf16[1024,3072]{1,0:T(8,128)(2,1)} %concatenate.10, s32[]{:T(128)S(6)} %select_n.23, f32[65,1536]{1,0:T(8,128)S(1)} %fusion.19, bf16[1024,64]{0,1:T(8,128)(2,1)S(1)} %copy-done.2), kind=kOutput, calls=%fused_computation.1 | convolution fusion | flops 1233123840 | bytes 9973764 | tf_op jit(solution)/shard_map/dot_general | solution.py:16
  168.6 3.0 %multiply_reduce_fusion.1 = (f32[640]{0:T(1024)S(1)}, f32[1024,640]{1,0:T(8,128)}) fusion(bf16[1024,640]{1,0:T(8,128)(2,1)S(1)} %copy-done.1, f32[65,640]{1,0:T(8,128)S(1)} %fusion.23, bf16[1024,64]{0,1:T(8,128)(2,1)S(1)} %copy-done.2), kind=kOutput, calls=%fused_computation.6 | convolution fusion | flops 513801600 | bytes 4232192 | tf_op jit(solution)/shard_map/dot_general | solution.py:16
  171.6 10.3 %all-reduce.1 = (f32[1536]{0:T(1024)S(1)}, f32[640]{0:T(1024)S(1)}) all-reduce(f32[1536]{0:T(1024)S(1)} %get-tuple-element.9, f32[640]{0:T(1024)S(1)} %get-tuple-element.11), channel_id=1, replica_groups=mesh['groups'=1,'samp'=4,'var'=8] {'samp'}, use_global_device_ids=true, to_apply=%region_8.9 | all-reduce | flops 2176 | bytes 17408 | tf_op jit(solution)/shard_map/psum | solution.py:39
  181.9 8.9 %fusion = f32[640,1536]{1,0:T(8,128)} fusion(f32[1024,1536]{1,0:T(8,128)} %get-tuple-element.10, f32[1536]{0:T(1024)S(1)} %add_rsqrt_fusion, bf16[1024,3072]{1,0:T(8,128)(2,1)} %concatenate.10, s32[]{:T(128)S(6)} %select_n.23, f32[1024,640]{1,0:T(8,128)} %get-tuple-element.12, bf16[1024,640]{1,0:T(8,128)(2,1)S(1)} %copy-done.1, f32[640]{0:T(1024)S(1)} %add_rsqrt_fusion.1), kind=kOutput, calls=%fused_computation.3 | convolution fusion | flops 2022178816 | bytes 17310212 | tf_op jit(solution)/shard_map/dot_general | solution.py:44
  193.0 41.2 %reduce-scatter.2.cloned.1.call-done = f32[160,1536]{1,0:T(8,128)} async-done(((f32[640,1536]{1,0:T(8,128)}), f32[160,1536]{1,0:T(8,128)}) %reduce-scatter.2.cloned.1.call-update) | async-done | bytes 983056 | tf_op jit(solution)/shard_map/reduce_scatter | solution.py:47
  234.2 2.3 fusion.6
  (37 shorter events, 4.6 us)
Async XLA Ops:
  6.5 184.3 %copy-start = (f32[5,16]{1,0:T(8,128)S(1)}, f32[5,16]{1,0:T(8,128)}, u32[]{:S(2)}) copy-start(f32[5,16]{1,0:T(8,128)} %param.11) | copy-start | bytes 964
  6.5 152.1 %all-reduce.5.cloned.1.call-start = ((), (), s32[]{:S(2)}) async-start(), calls=%async_computation.2 | async-start | bytes 1253376 | tf_op jit(solution)/shard_map/psum | solution.py:34
  7.8 18.0 %collective-permute-start = (bf16[1024,192]{1,0:T(8,128)(2,1)S(1)}, bf16[1024,192]{1,0:T(8,128)(2,1)S(1)}, u32[]{:S(2)}, u32[]{:S(2)}) collective-permute-start(bf16[1024,192]{1,0:T(8,128)(2,1)S(1)} %copy.23), channel_id=1, source_target_pairs={{0,1},{1,2},{2,3},{3,4},{4,5},{5,6},{6,7},{7,0},{8,9},{9,10},{10,1... | collective-permute-start | bytes 1179656 | tf_op jit(solution)/shard_map/ppermute | solution.py:26
  25.8 15.8 %collective-permute-start.1 = (bf16[1024,192]{1,0:T(8,128)(2,1)S(1)}, bf16[1024,192]{1,0:T(8,128)(2,1)S(1)}, u32[]{:S(2)}, u32[]{:S(2)}) collective-permute-start(bf16[1024,192]{1,0:T(8,128)(2,1)S(1)} %collective-permute-done), channel_id=1, source_target_pairs={{0,1},{1,2},{2,3},{3,4},{4,5},{5,6},{6,7},{7,0},{8,9},{9,10},{10,1... | collective-permute-start | bytes 1179656 | tf_op jit(solution)/shard_map/ppermute | solution.py:26
  41.5 14.9 %collective-permute-start.2 = (bf16[1024,192]{1,0:T(8,128)(2,1)S(1)}, bf16[1024,192]{1,0:T(8,128)(2,1)S(1)}, u32[]{:S(2)}, u32[]{:S(2)}) collective-permute-start(bf16[1024,192]{1,0:T(8,128)(2,1)S(1)} %collective-permute-done.1), channel_id=1, source_target_pairs={{0,1},{1,2},{2,3},{3,4},{4,5},{5,6},{6,7},{7,0},{8,9},{9,10},{10,1... | collective-permute-start | bytes 1179656 | tf_op jit(solution)/shard_map/ppermute | solution.py:26
  56.5 14.1 %collective-permute-start.3 = (bf16[1024,192]{1,0:T(8,128)(2,1)S(1)}, bf16[1024,192]{1,0:T(8,128)(2,1)S(1)}, u32[]{:S(2)}, u32[]{:S(2)}) collective-permute-start(bf16[1024,192]{1,0:T(8,128)(2,1)S(1)} %collective-permute-done.2), channel_id=1, source_target_pairs={{0,1},{1,2},{2,3},{3,4},{4,5},{5,6},{6,7},{7,0},{8,9},{9,10},{10,1... | collective-permute-start | bytes 1179656 | tf_op jit(solution)/shard_map/ppermute | solution.py:26
  70.6 13.2 %collective-permute-start.4 = (bf16[1024,192]{1,0:T(8,128)(2,1)S(1)}, bf16[1024,192]{1,0:T(8,128)(2,1)S(1)}, u32[]{:S(2)}, u32[]{:S(2)}) collective-permute-start(bf16[1024,192]{1,0:T(8,128)(2,1)S(1)} %collective-permute-done.3), channel_id=1, source_target_pairs={{0,1},{1,2},{2,3},{3,4},{4,5},{5,6},{6,7},{7,0},{8,9},{9,10},{10,1... | collective-permute-start | bytes 1179656 | tf_op jit(solution)/shard_map/ppermute | solution.py:26
  83.8 12.5 %collective-permute-start.5 = (bf16[1024,192]{1,0:T(8,128)(2,1)S(1)}, bf16[1024,192]{1,0:T(8,128)(2,1)}, u32[]{:S(2)}, u32[]{:S(2)}) collective-permute-start(bf16[1024,192]{1,0:T(8,128)(2,1)S(1)} %collective-permute-done.4), channel_id=1, source_target_pairs={{0,1},{1,2},{2,3},{3,4},{4,5},{5,6},{6,7},{7,0},{8,9},{9,10},{10,1... | collective-permute-start | bytes 1179656 | tf_op jit(solution)/shard_map/ppermute | solution.py:26
  96.2 16.3 %collective-permute-start.6 = (bf16[1024,192]{1,0:T(8,128)(2,1)}, bf16[1024,192]{1,0:T(8,128)(2,1)}, u32[]{:S(2)}, u32[]{:S(2)}) collective-permute-start(bf16[1024,192]{1,0:T(8,128)(2,1)} %collective-permute-done.5), channel_id=1, source_target_pairs={{0,1},{1,2},{2,3},{3,4},{4,5},{5,6},{6,7},{7,0},{8,9},{9,10},{10,1... | collective-permute-start | bytes 1179656 | tf_op jit(solution)/shard_map/ppermute | solution.py:26
  104.7 18.4 %copy-start.2 = (bf16[1024,64]{0,1:T(8,128)(2,1)S(1)}, bf16[1024,64]{0,1:T(8,128)(2,1)}, u32[]{:S(2)}) copy-start(bf16[1024,64]{0,1:T(8,128)(2,1)} %param.8) | copy-start | bytes 393220
  127.0 107.2 %reduce-scatter.2.cloned.1.call-start = ((), (), s32[]{:S(2)}) async-start(), calls=%async_computation.1 | async-start | bytes 4915200 | tf_op jit(solution)/shard_map/reduce_scatter | solution.py:47
  160.7 7.1 %copy-start.3 = (f32[65,640]{1,0:T(8,128)S(1)}, f32[65,640]{1,0:T(8,128)}, u32[]{:S(2)}) copy-start(f32[65,640]{1,0:T(8,128)} %get-tuple-element.8) | copy-start | bytes 499204
  160.7 7.8 %copy-start.1 = (bf16[1024,640]{1,0:T(8,128)(2,1)S(1)}, bf16[1024,640]{1,0:T(8,128)(2,1)}, u32[]{:S(2)}) copy-start(bf16[1024,640]{1,0:T(8,128)(2,1)} %param.6) | copy-start | bytes 3932164
  190.8 0.7 copy-start.5
  190.8 0.9 copy-start.4
Sparse Core Ops, SparseCore 0:
  127.1 31.4 all-reduce.4
  190.9 43.2 reduce-scatter.1
